TPU v7x, 32 devices: a whole 2x2x4 slice. The times are simulated.
32 devices in a mesh: dom: 32 (over z, y, x, core).
Axes of the slice: x: 2, y: 2, z: 4, core: 2. Of those that a mesh axis runs over, the one named last changes fastest.
Arguments:
- grad_out: bfloat16 [16384, 256], P('dom'), may hold values from -6 to 6
- states: bfloat16 [16384, 256], P('dom'), may hold values from -0.98828125 to 0.98828125
- slopes: bfloat16 [16384, 256], P('dom'), may hold values from 0.099609375 to 1
- weight: bfloat16 [256, 256], replicated, may hold values from -0.375 to 0.375
- tiles: bfloat16 [768, 128, 128], P('dom'), may hold values from -0.23925781 to 0.23925781
- tile_dst: int32 [768], P('dom'), may hold values from 0 to 3, as said below
- tile_src: int32 [768], P('dom'), may hold values from 0 to 7, as said below
- tile_count: int32 [32], P('dom'), may hold values from 12 to 24, as said below
- send_rows: int32 [128, 128], P('dom'), may hold values from 0 to 511, as said below
Outputs:
- adjoint: float32 [16384, 256], P('dom')
- weight_grad: float32 [256, 256], replicated
Inputs may be any that keep to these rules, and one draw needn't show every extreme that they name: `tile_src`: slot s of a partition with s < 4 has source tile 4 + s; slots 4 to 7 have destination and source tile s - 4; other used slots name a destination below 4 and a source below 8. `tile_dst`: destination tiles of a partition's slots. `tile_count`: some partition uses all 24 slots. `send_rows`: each list holds distinct local rows.
All inputs are finite; a program needn't handle non-finite values.
Results may differ from a plain program's by a relative error of at most 0.009.
Values may be sent and summed in bfloat16 or wider, within the bound.
No kernel may reach another device: no remote copies, remote signals or barrier semaphores. Data moves between devices by JAX's collectives and lax.ppermute only.
A program may use at most 64 MiB of HBM per device.

v0:
```python
import jax
import jax.numpy as jnp
from jax import lax
from jax.sharding import PartitionSpec as P

ITERS = 4
neighbour_steps = (1, -1, 16, -16)


def passed_along(value, axis, steps):
    count = lax.axis_size(axis)
    pairs = [(source, (source + steps) % count) for source in range(count)]
    return lax.ppermute(value, axis, pairs)


def add_tiles(tiles, tile_dst, tile_src, count, extended, total, keep):
    size = tiles.shape[1]
    width = extended.shape[1]
    sources = extended.shape[0] // size
    blocks = total.shape[0] // size
    slots = tiles.shape[0]
    stacked = extended.reshape(sources, size, width)
    index = jnp.minimum(tile_src, sources - 1)
    rows = jnp.take(stacked, index, axis=0)
    prod = jnp.einsum("tij,tjh->tih", tiles, rows, preferred_element_type=jnp.float32)
    used = (jnp.arange(slots, dtype=jnp.int32) < count) & keep(tile_src)
    onehot = (
        (tile_dst[None, :] == jnp.arange(blocks, dtype=jnp.int32)[:, None]) & used[None, :]
    ).astype(jnp.float32)
    summed = jnp.dot(onehot, prod.reshape(slots, size * width), precision=lax.Precision.HIGHEST)
    return summed.reshape(blocks * size, width)


def with_boundary(scaled, send_rows):
    pieces = [scaled]
    for direction in range(4):
        chosen = jnp.take(scaled, send_rows[direction], axis=0)
        pieces.append(passed_along(chosen, "dom", neighbour_steps[direction]))
    return jnp.concatenate(pieces, axis=0)


def propagate(scaled, tiles, tile_dst, tile_src, count, send_rows):
    empty = jnp.zeros(scaled.shape, jnp.float32)
    extended = with_boundary(scaled, send_rows)
    return add_tiles(tiles, tile_dst, tile_src, count, extended, empty, lambda s: s >= 0)


def per_device(grad_out, states, slopes, weight, tiles, tile_dst, tile_src, tile_count, send_rows):
    count = tile_count[0]
    slope_values = slopes.astype(jnp.float32)
    base = grad_out.astype(jnp.float32)
    adjoint = base
    for step in range(ITERS):
        scaled = (slope_values * adjoint).astype(jnp.bfloat16)
        mixed = propagate(scaled, tiles, tile_dst, tile_src, count, send_rows).astype(jnp.bfloat16)
        adjoint = base + lax.dot_general(
            mixed, weight, (((1,), (1,)), ((), ())), preferred_element_type=jnp.float32
        )
    final_scaled = (slope_values * adjoint).astype(jnp.bfloat16)
    node_total = lax.axis_size("dom") * grad_out.shape[0]
    factor = 1.0 / jnp.sqrt(jnp.float32(node_total))
    state_values = states.astype(jnp.float32)
    final_mixed = propagate(final_scaled, tiles, tile_dst, tile_src, count, send_rows)
    grad = lax.psum(
        lax.dot_general(
            state_values, final_mixed, (((0,), (0,)), ((), ())), precision=lax.Precision.HIGHEST
        )
        * factor,
        "dom",
    )
    return (adjoint, grad)


def solution(mesh):
    in_specs = (
        P("dom", None),
        P("dom", None),
        P("dom", None),
        P(),
        P("dom", None, None),
        P("dom"),
        P("dom"),
        P("dom"),
        P("dom", None),
    )
    out_specs = (P("dom", None), P())
    return jax.shard_map(
        per_device, mesh=mesh, in_specs=in_specs, out_specs=out_specs, check_vma=False
    )
```

profile of v0, /device:TPU:0, one launch (start us, length us, event | category | flops | bytes accessed | tf_op | source)
XLA Modules:
  0.0 283.6 jit_solution(12685391604185503891)
XLA Ops:
  10.1 6.5 %collective-permute-start.1 = (bf16[128,256]{1,0:T(8,128)(2,1)S(1)}, bf16[128,256]{1,0:T(8,128)(2,1)S(1)}, u32[]{:S(2)}, u32[]{:S(2)}) collective-permute-start(bf16[128,256]{1,0:T(8,128)(2,1)S(1)} %broadcast_select_fusion.14), channel_id=1, source_target_pairs={{0,31},{1,0},{2,1},{3,2},{4,3},{5,4},{6,5},{7,6},{8,7},{9,8},{10,9... | collective-permute-start | bytes 196616 | tf_op jit(solution)/shard_map/ppermute | solution.py:13
  19.6 3.0 %collective-permute-start.3 = (bf16[128,256]{1,0:T(8,128)(2,1)S(1)}, bf16[128,256]{1,0:T(8,128)(2,1)S(1)}, u32[]{:S(2)}, u32[]{:S(2)}) collective-permute-start(bf16[128,256]{1,0:T(8,128)(2,1)S(1)} %broadcast_select_fusion.4), channel_id=1, source_target_pairs={{0,16},{1,17},{2,18},{3,19},{4,20},{5,21},{6,22},{7,23},{8,24},{9,... | collective-permute-start | bytes 196616 | tf_op jit(solution)/shard_map/ppermute | solution.py:13
  26.6 2.3 convolution_bitcast_fusion.4
  28.9 3.6 %copy.28 = f32[3,8,128,256]{3,1,2,0:T(8,128)} copy(f32[3,8,128,256]{2,3,1,0:T(8,128)} %bitcast.77) | data formatting | bytes 6291456
  32.5 3.1 %convolution_convert_fusion.3 = bf16[4,32768]{1,0:T(4,128)(2,1)S(1)} fusion(pred[4,24]{1,0:T(4,128)(4,1)S(1)} %fusion.24, f32[24,32768]{1,0:T(8,128)} %bitcast.71), kind=kOutput, calls=%fused_computation.28 | convolution fusion | flops 37879808 | bytes 3407968 | tf_op jit(solution)/shard_map/dot_general | solution.py:30
  39.9 5.4 %collective-permute-start.5 = (bf16[128,256]{1,0:T(8,128)(2,1)S(1)}, bf16[128,256]{1,0:T(8,128)(2,1)S(1)}, u32[]{:S(2)}, u32[]{:S(2)}) collective-permute-start(bf16[128,256]{1,0:T(8,128)(2,1)S(1)} %broadcast_select_fusion.13), channel_id=1, source_target_pairs={{0,31},{1,0},{2,1},{3,2},{4,3},{5,4},{6,5},{7,6},{8,7},{9,8},{10,9... | collective-permute-start | bytes 196616 | tf_op jit(solution)/shard_map/ppermute | solution.py:13
  45.4 2.9 %collective-permute-start.7 = (bf16[128,256]{1,0:T(8,128)(2,1)S(1)}, bf16[128,256]{1,0:T(8,128)(2,1)S(1)}, u32[]{:S(2)}, u32[]{:S(2)}) collective-permute-start(bf16[128,256]{1,0:T(8,128)(2,1)S(1)} %broadcast_select_fusion.3), channel_id=1, source_target_pairs={{0,16},{1,17},{2,18},{3,19},{4,20},{5,21},{6,22},{7,23},{8,24},{9,... | collective-permute-start | bytes 196616 | tf_op jit(solution)/shard_map/ppermute | solution.py:13
  48.3 2.8 collective-permute-done.6
  51.8 1.9 gather_fusion.9
  53.6 3.7 %convolution_bitcast_fusion.3 = f32[24,128,256]{1,2,0:T(8,128)} fusion(bf16[24,128,128]{2,1,0:T(8,128)(2,1)S(1)} %copy-done, bf16[24,128,256]{2,1,0:T(8,128)(2,1)} %gather_fusion.9, pred[24]{0:T(512)(128)(4,1)S(1)} %get-tuple-element.10), kind=kOutput, calls=%fused_computation.32 | convolution fusion | flops 202113024 | bytes 5505048 | tf_op jit(solution)/shard_map/tij,tjh->tih/dot_general | solution.py:25
  57.4 3.6 %copy.29 = f32[3,8,128,256]{3,1,2,0:T(8,128)} copy(f32[3,8,128,256]{2,3,1,0:T(8,128)} %bitcast.78) | data formatting | bytes 6291456
  60.9 3.1 %convolution_convert_fusion.2 = bf16[4,32768]{1,0:T(4,128)(2,1)S(1)} fusion(pred[4,24]{1,0:T(4,128)(4,1)S(1)} %fusion.24, f32[24,32768]{1,0:T(8,128)} %bitcast.72), kind=kOutput, calls=%fused_computation.27 | convolution fusion | flops 37879808 | bytes 3407968 | tf_op jit(solution)/shard_map/dot_general | solution.py:30
  68.3 5.6 %collective-permute-start.9 = (bf16[128,256]{1,0:T(8,128)(2,1)S(1)}, bf16[128,256]{1,0:T(8,128)(2,1)S(1)}, u32[]{:S(2)}, u32[]{:S(2)}) collective-permute-start(bf16[128,256]{1,0:T(8,128)(2,1)S(1)} %broadcast_select_fusion.12), channel_id=1, source_target_pairs={{0,31},{1,0},{2,1},{3,2},{4,3},{5,4},{6,5},{7,6},{8,7},{9,8},{10,9... | collective-permute-start | bytes 196616 | tf_op jit(solution)/shard_map/ppermute | solution.py:13
  73.9 2.9 %collective-permute-start.11 = (bf16[128,256]{1,0:T(8,128)(2,1)S(1)}, bf16[128,256]{1,0:T(8,128)(2,1)S(1)}, u32[]{:S(2)}, u32[]{:S(2)}) collective-permute-start(bf16[128,256]{1,0:T(8,128)(2,1)S(1)} %broadcast_select_fusion.2), channel_id=1, source_target_pairs={{0,16},{1,17},{2,18},{3,19},{4,20},{5,21},{6,22},{7,23},{8,24},{9,... | collective-permute-start | bytes 196616 | tf_op jit(solution)/shard_map/ppermute | solution.py:13
  76.8 2.2 collective-permute-done.10
  79.7 1.9 gather_fusion.14
  81.6 3.7 %convolution_bitcast_fusion.2 = f32[24,128,256]{1,2,0:T(8,128)} fusion(bf16[24,128,128]{2,1,0:T(8,128)(2,1)S(1)} %copy-done, bf16[24,128,256]{2,1,0:T(8,128)(2,1)} %gather_fusion.14, pred[24]{0:T(512)(128)(4,1)S(1)} %get-tuple-element.10), kind=kOutput, calls=%fused_computation.31 | convolution fusion | flops 202113024 | bytes 5505048 | tf_op jit(solution)/shard_map/tij,tjh->tih/dot_general | solution.py:25
  85.3 3.6 %copy.30 = f32[3,8,128,256]{3,1,2,0:T(8,128)} copy(f32[3,8,128,256]{2,3,1,0:T(8,128)} %bitcast.79) | data formatting | bytes 6291456
  88.9 3.1 %convolution_convert_fusion.1 = bf16[4,32768]{1,0:T(4,128)(2,1)S(1)} fusion(pred[4,24]{1,0:T(4,128)(4,1)S(1)} %fusion.24, f32[24,32768]{1,0:T(8,128)} %bitcast.73), kind=kOutput, calls=%fused_computation.26 | convolution fusion | flops 37879808 | bytes 3407968 | tf_op jit(solution)/shard_map/dot_general | solution.py:30
  96.2 5.4 %collective-permute-start.13 = (bf16[128,256]{1,0:T(8,128)(2,1)S(1)}, bf16[128,256]{1,0:T(8,128)(2,1)S(1)}, u32[]{:S(2)}, u32[]{:S(2)}) collective-permute-start(bf16[128,256]{1,0:T(8,128)(2,1)S(1)} %broadcast_select_fusion.11), channel_id=1, source_target_pairs={{0,31},{1,0},{2,1},{3,2},{4,3},{5,4},{6,5},{7,6},{8,7},{9,8},{10,9... | collective-permute-start | bytes 196616 | tf_op jit(solution)/shard_map/ppermute | solution.py:13
  102.1 2.5 collective-permute-start.15
  104.6 2.2 collective-permute-done.14
  109.4 3.7 %convolution_bitcast_fusion.1 = f32[24,128,256]{1,2,0:T(8,128)} fusion(bf16[24,128,128]{2,1,0:T(8,128)(2,1)S(1)} %copy-done, bf16[24,128,256]{2,1,0:T(8,128)(2,1)} %gather_fusion.19, pred[24]{0:T(512)(128)(4,1)S(1)} %get-tuple-element.10), kind=kOutput, calls=%fused_computation.30 | convolution fusion | flops 202113024 | bytes 5505048 | tf_op jit(solution)/shard_map/tij,tjh->tih/dot_general | solution.py:25
  113.1 3.6 %copy.31 = f32[3,8,128,256]{3,1,2,0:T(8,128)} copy(f32[3,8,128,256]{2,3,1,0:T(8,128)} %bitcast.80) | data formatting | bytes 6291456
  116.7 3.1 %convolution_convert_fusion = bf16[4,32768]{1,0:T(4,128)(2,1)S(1)} fusion(pred[4,24]{1,0:T(4,128)(4,1)S(1)} %fusion.24, f32[24,32768]{1,0:T(8,128)} %bitcast.74), kind=kOutput, calls=%fused_computation.25 | convolution fusion | flops 37879808 | bytes 3407968 | tf_op jit(solution)/shard_map/dot_general | solution.py:30
  124.8 5.6 %collective-permute-start.17 = (bf16[128,256]{1,0:T(8,128)(2,1)S(1)}, bf16[128,256]{1,0:T(8,128)(2,1)S(1)}, u32[]{:S(2)}, u32[]{:S(2)}) collective-permute-start(bf16[128,256]{1,0:T(8,128)(2,1)S(1)} %broadcast_select_fusion.10), channel_id=1, source_target_pairs={{0,31},{1,0},{2,1},{3,2},{4,3},{5,4},{6,5},{7,6},{8,7},{9,8},{10,9... | collective-permute-start | bytes 196616 | tf_op jit(solution)/shard_map/ppermute | solution.py:13
  130.8 2.5 collective-permute-start.19
  133.4 2.2 collective-permute-done.18
  138.1 3.7 %convolution_bitcast_fusion = f32[24,128,256]{1,2,0:T(8,128)} fusion(bf16[24,128,128]{2,1,0:T(8,128)(2,1)S(1)} %copy-done, bf16[24,128,256]{2,1,0:T(8,128)(2,1)} %gather_fusion.24, pred[24]{0:T(512)(128)(4,1)S(1)} %get-tuple-element.10), kind=kOutput, calls=%fused_computation.29 | convolution fusion | flops 202113024 | bytes 5505048 | tf_op jit(solution)/shard_map/tij,tjh->tih/dot_general | solution.py:25
  141.9 3.6 %copy.32 = f32[3,8,128,256]{3,1,2,0:T(8,128)} copy(f32[3,8,128,256]{2,3,1,0:T(8,128)} %bitcast.75) | data formatting | bytes 6291456
  145.4 3.1 %fusion.32 = f32[4,32768]{1,0:T(4,128)S(1)} fusion(pred[4,24]{1,0:T(4,128)(4,1)S(1)} %fusion.24, f32[24,32768]{1,0:T(8,128)} %bitcast.76), kind=kOutput, calls=%fused_computation.133 | convolution fusion | flops 37748736 | bytes 3670112 | tf_op jit(solution)/shard_map/dot_general | solution.py:30
  150.2 124.7 %all-reduce.2.cloned.1.call-done = f32[256,256]{0,1:T(8,128)} async-done(((f32[256,256]{0,1:T(8,128)}), f32[256,256]{0,1:T(8,128)}) %all-reduce.2.cloned.1.call-update) | async-done | bytes 262160 | tf_op jit(solution)/shard_map/psum | solution.py:64
  (125 shorter events, 37.8 us)
Async XLA Ops:
  7.2 19.4 %copy-start = (bf16[24,128,128]{2,1,0:T(8,128)(2,1)S(1)}, bf16[24,128,128]{2,1,0:T(8,128)(2,1)}, u32[]{:S(2)}) copy-start(bf16[24,128,128]{2,1,0:T(8,128)(2,1)} %param.17) | copy-start | bytes 2359300
  7.2 267.8 %all-reduce.2.cloned.1.call-start = ((), (), s32[]{:S(2)}) async-start(), calls=%async_computation | async-start | bytes 524288 | tf_op jit(solution)/shard_map/psum | solution.py:64
  9.2 14.0 %copy-start.5 = (s32[24]{0:T(128)S(1)}, s32[24]{0:T(128)}, u32[]{:S(2)}) copy-start(s32[24]{0:T(128)} %param.19) | copy-start | bytes 292
  9.2 14.1 %copy-start.6 = (s32[24]{0:T(128)S(1)}, s32[24]{0:T(128)}, u32[]{:S(2)}) copy-start(s32[24]{0:T(128)} %param.18) | copy-start | bytes 292
  10.1 14.8 %collective-permute-start.1 = (bf16[128,256]{1,0:T(8,128)(2,1)S(1)}, bf16[128,256]{1,0:T(8,128)(2,1)S(1)}, u32[]{:S(2)}, u32[]{:S(2)}) collective-permute-start(bf16[128,256]{1,0:T(8,128)(2,1)S(1)} %broadcast_select_fusion.14), channel_id=1, source_target_pairs={{0,31},{1,0},{2,1},{3,2},{4,3},{5,4},{6,5},{7,6},{8,7},{9,8},{10,9... | collective-permute-start | bytes 196616 | tf_op jit(solution)/shard_map/ppermute | solution.py:13
  17.5 7.4 %collective-permute-start = (bf16[128,256]{1,0:T(8,128)(2,1)S(1)}, bf16[128,256]{1,0:T(8,128)(2,1)S(1)}, u32[]{:S(2)}, u32[]{:S(2)}) collective-permute-start(bf16[128,256]{1,0:T(8,128)(2,1)S(1)} %broadcast_select_fusion.19), channel_id=1, source_target_pairs={{0,1},{1,2},{2,3},{3,4},{4,5},{5,6},{6,7},{7,8},{8,9},{9,10},{10,1... | collective-permute-start | bytes 196616 | tf_op jit(solution)/shard_map/ppermute | solution.py:13
  18.6 6.4 %collective-permute-start.2 = (bf16[128,256]{1,0:T(8,128)(2,1)S(1)}, bf16[128,256]{1,0:T(8,128)(2,1)S(1)}, u32[]{:S(2)}, u32[]{:S(2)}) collective-permute-start(bf16[128,256]{1,0:T(8,128)(2,1)S(1)} %broadcast_select_fusion.9), channel_id=1, source_target_pairs={{0,16},{1,17},{2,18},{3,19},{4,20},{5,21},{6,22},{7,23},{8,24},{9,... | collective-permute-start | bytes 196616 | tf_op jit(solution)/shard_map/ppermute | solution.py:13
  19.6 6.3 %collective-permute-start.3 = (bf16[128,256]{1,0:T(8,128)(2,1)S(1)}, bf16[128,256]{1,0:T(8,128)(2,1)S(1)}, u32[]{:S(2)}, u32[]{:S(2)}) collective-permute-start(bf16[128,256]{1,0:T(8,128)(2,1)S(1)} %broadcast_select_fusion.4), channel_id=1, source_target_pairs={{0,16},{1,17},{2,18},{3,19},{4,20},{5,21},{6,22},{7,23},{8,24},{9,... | collective-permute-start | bytes 196616 | tf_op jit(solution)/shard_map/ppermute | solution.py:13
  32.5 3.3 %copy-start.1 = (bf16[512,256]{1,0:T(8,128)(2,1)S(1)}, bf16[512,256]{1,0:T(8,128)(2,1)}, u32[]{:S(2)}) copy-start(bf16[512,256]{1,0:T(8,128)(2,1)} %param.15) | copy-start | bytes 786436
  32.5 3.3 %copy-start.2 = (bf16[512,256]{1,0:T(8,128)(2,1)S(1)}, bf16[512,256]{1,0:T(8,128)(2,1)}, u32[]{:S(2)}) copy-start(bf16[512,256]{1,0:T(8,128)(2,1)} %param.13) | copy-start | bytes 786436
  32.5 3.4 %copy-start.3 = (bf16[256,256]{1,0:T(8,128)(2,1)S(1)}, bf16[256,256]{1,0:T(8,128)(2,1)}, u32[]{:S(2)}) copy-start(bf16[256,256]{1,0:T(8,128)(2,1)} %param.16) | copy-start | bytes 393220
  39.8 8.5 %collective-permute-start.4 = (bf16[128,256]{1,0:T(8,128)(2,1)S(1)}, bf16[128,256]{1,0:T(8,128)(2,1)S(1)}, u32[]{:S(2)}, u32[]{:S(2)}) collective-permute-start(bf16[128,256]{1,0:T(8,128)(2,1)S(1)} %broadcast_select_fusion.18), channel_id=1, source_target_pairs={{0,1},{1,2},{2,3},{3,4},{4,5},{5,6},{6,7},{7,8},{8,9},{9,10},{10,1... | collective-permute-start | bytes 196616 | tf_op jit(solution)/shard_map/ppermute | solution.py:13
  39.9 8.3 %collective-permute-start.5 = (bf16[128,256]{1,0:T(8,128)(2,1)S(1)}, bf16[128,256]{1,0:T(8,128)(2,1)S(1)}, u32[]{:S(2)}, u32[]{:S(2)}) collective-permute-start(bf16[128,256]{1,0:T(8,128)(2,1)S(1)} %broadcast_select_fusion.13), channel_id=1, source_target_pairs={{0,31},{1,0},{2,1},{3,2},{4,3},{5,4},{6,5},{7,6},{8,7},{9,8},{10,9... | collective-permute-start | bytes 196616 | tf_op jit(solution)/shard_map/ppermute | solution.py:13
  45.3 5.7 %collective-permute-start.6 = (bf16[128,256]{1,0:T(8,128)(2,1)S(1)}, bf16[128,256]{1,0:T(8,128)(2,1)S(1)}, u32[]{:S(2)}, u32[]{:S(2)}) collective-permute-start(bf16[128,256]{1,0:T(8,128)(2,1)S(1)} %broadcast_select_fusion.8), channel_id=1, source_target_pairs={{0,16},{1,17},{2,18},{3,19},{4,20},{5,21},{6,22},{7,23},{8,24},{9,... | collective-permute-start | bytes 196616 | tf_op jit(solution)/shard_map/ppermute | solution.py:13
  45.4 6.4 %collective-permute-start.7 = (bf16[128,256]{1,0:T(8,128)(2,1)S(1)}, bf16[128,256]{1,0:T(8,128)(2,1)S(1)}, u32[]{:S(2)}, u32[]{:S(2)}) collective-permute-start(bf16[128,256]{1,0:T(8,128)(2,1)S(1)} %broadcast_select_fusion.3), channel_id=1, source_target_pairs={{0,16},{1,17},{2,18},{3,19},{4,20},{5,21},{6,22},{7,23},{8,24},{9,... | collective-permute-start | bytes 196616 | tf_op jit(solution)/shard_map/ppermute | solution.py:13
  68.1 8.6 %collective-permute-start.8 = (bf16[128,256]{1,0:T(8,128)(2,1)S(1)}, bf16[128,256]{1,0:T(8,128)(2,1)S(1)}, u32[]{:S(2)}, u32[]{:S(2)}) collective-permute-start(bf16[128,256]{1,0:T(8,128)(2,1)S(1)} %broadcast_select_fusion.17), channel_id=1, source_target_pairs={{0,1},{1,2},{2,3},{3,4},{4,5},{5,6},{6,7},{7,8},{8,9},{9,10},{10,1... | collective-permute-start | bytes 196616 | tf_op jit(solution)/shard_map/ppermute | solution.py:13
  68.3 8.5 %collective-permute-start.9 = (bf16[128,256]{1,0:T(8,128)(2,1)S(1)}, bf16[128,256]{1,0:T(8,128)(2,1)S(1)}, u32[]{:S(2)}, u32[]{:S(2)}) collective-permute-start(bf16[128,256]{1,0:T(8,128)(2,1)S(1)} %broadcast_select_fusion.12), channel_id=1, source_target_pairs={{0,31},{1,0},{2,1},{3,2},{4,3},{5,4},{6,5},{7,6},{8,7},{9,8},{10,9... | collective-permute-start | bytes 196616 | tf_op jit(solution)/shard_map/ppermute | solution.py:13
  73.9 5.2 %collective-permute-start.10 = (bf16[128,256]{1,0:T(8,128)(2,1)S(1)}, bf16[128,256]{1,0:T(8,128)(2,1)S(1)}, u32[]{:S(2)}, u32[]{:S(2)}) collective-permute-start(bf16[128,256]{1,0:T(8,128)(2,1)S(1)} %broadcast_select_fusion.7), channel_id=1, source_target_pairs={{0,16},{1,17},{2,18},{3,19},{4,20},{5,21},{6,22},{7,23},{8,24},{9,... | collective-permute-start | bytes 196616 | tf_op jit(solution)/shard_map/ppermute | solution.py:13
  73.9 5.9 %collective-permute-start.11 = (bf16[128,256]{1,0:T(8,128)(2,1)S(1)}, bf16[128,256]{1,0:T(8,128)(2,1)S(1)}, u32[]{:S(2)}, u32[]{:S(2)}) collective-permute-start(bf16[128,256]{1,0:T(8,128)(2,1)S(1)} %broadcast_select_fusion.2), channel_id=1, source_target_pairs={{0,16},{1,17},{2,18},{3,19},{4,20},{5,21},{6,22},{7,23},{8,24},{9,... | collective-permute-start | bytes 196616 | tf_op jit(solution)/shard_map/ppermute | solution.py:13
  96.1 8.5 %collective-permute-start.12 = (bf16[128,256]{1,0:T(8,128)(2,1)S(1)}, bf16[128,256]{1,0:T(8,128)(2,1)S(1)}, u32[]{:S(2)}, u32[]{:S(2)}) collective-permute-start(bf16[128,256]{1,0:T(8,128)(2,1)S(1)} %broadcast_select_fusion.16), channel_id=1, source_target_pairs={{0,1},{1,2},{2,3},{3,4},{4,5},{5,6},{6,7},{7,8},{8,9},{9,10},{10,1... | collective-permute-start | bytes 196616 | tf_op jit(solution)/shard_map/ppermute | solution.py:13
  96.2 8.3 %collective-permute-start.13 = (bf16[128,256]{1,0:T(8,128)(2,1)S(1)}, bf16[128,256]{1,0:T(8,128)(2,1)S(1)}, u32[]{:S(2)}, u32[]{:S(2)}) collective-permute-start(bf16[128,256]{1,0:T(8,128)(2,1)S(1)} %broadcast_select_fusion.11), channel_id=1, source_target_pairs={{0,31},{1,0},{2,1},{3,2},{4,3},{5,4},{6,5},{7,6},{8,7},{9,8},{10,9... | collective-permute-start | bytes 196616 | tf_op jit(solution)/shard_map/ppermute | solution.py:13
  101.6 5.2 %collective-permute-start.14 = (bf16[128,256]{1,0:T(8,128)(2,1)S(1)}, bf16[128,256]{1,0:T(8,128)(2,1)S(1)}, u32[]{:S(2)}, u32[]{:S(2)}) collective-permute-start(bf16[128,256]{1,0:T(8,128)(2,1)S(1)} %broadcast_select_fusion.6), channel_id=1, source_target_pairs={{0,16},{1,17},{2,18},{3,19},{4,20},{5,21},{6,22},{7,23},{8,24},{9,... | collective-permute-start | bytes 196616 | tf_op jit(solution)/shard_map/ppermute | solution.py:13
  102.1 5.4 %collective-permute-start.15 = (bf16[128,256]{1,0:T(8,128)(2,1)S(1)}, bf16[128,256]{1,0:T(8,128)(2,1)S(1)}, u32[]{:S(2)}, u32[]{:S(2)}) collective-permute-start(bf16[128,256]{1,0:T(8,128)(2,1)S(1)} %broadcast_select_fusion.1), channel_id=1, source_target_pairs={{0,16},{1,17},{2,18},{3,19},{4,20},{5,21},{6,22},{7,23},{8,24},{9,... | collective-permute-start | bytes 196616 | tf_op jit(solution)/shard_map/ppermute | solution.py:13
  124.6 8.7 %collective-permute-start.16 = (bf16[128,256]{1,0:T(8,128)(2,1)S(1)}, bf16[128,256]{1,0:T(8,128)(2,1)S(1)}, u32[]{:S(2)}, u32[]{:S(2)}) collective-permute-start(bf16[128,256]{1,0:T(8,128)(2,1)S(1)} %broadcast_select_fusion.15), channel_id=1, source_target_pairs={{0,1},{1,2},{2,3},{3,4},{4,5},{5,6},{6,7},{7,8},{8,9},{9,10},{10,1... | collective-permute-start | bytes 196616 | tf_op jit(solution)/shard_map/ppermute | solution.py:13
  124.8 8.5 %collective-permute-start.17 = (bf16[128,256]{1,0:T(8,128)(2,1)S(1)}, bf16[128,256]{1,0:T(8,128)(2,1)S(1)}, u32[]{:S(2)}, u32[]{:S(2)}) collective-permute-start(bf16[128,256]{1,0:T(8,128)(2,1)S(1)} %broadcast_select_fusion.10), channel_id=1, source_target_pairs={{0,31},{1,0},{2,1},{3,2},{4,3},{5,4},{6,5},{7,6},{8,7},{9,8},{10,9... | collective-permute-start | bytes 196616 | tf_op jit(solution)/shard_map/ppermute | solution.py:13
  130.4 5.2 %collective-permute-start.18 = (bf16[128,256]{1,0:T(8,128)(2,1)S(1)}, bf16[128,256]{1,0:T(8,128)(2,1)S(1)}, u32[]{:S(2)}, u32[]{:S(2)}) collective-permute-start(bf16[128,256]{1,0:T(8,128)(2,1)S(1)} %broadcast_select_fusion.5), channel_id=1, source_target_pairs={{0,16},{1,17},{2,18},{3,19},{4,20},{5,21},{6,22},{7,23},{8,24},{9,... | collective-permute-start | bytes 196616 | tf_op jit(solution)/shard_map/ppermute | solution.py:13
  130.8 5.4 %collective-permute-start.19 = (bf16[128,256]{1,0:T(8,128)(2,1)S(1)}, bf16[128,256]{1,0:T(8,128)(2,1)S(1)}, u32[]{:S(2)}, u32[]{:S(2)}) collective-permute-start(bf16[128,256]{1,0:T(8,128)(2,1)S(1)} %broadcast_select_fusion), channel_id=1, source_target_pairs={{0,16},{1,17},{2,18},{3,19},{4,20},{5,21},{6,22},{7,23},{8,24},{9,... | collective-permute-start | bytes 196616 | tf_op jit(solution)/shard_map/ppermute | solution.py:13
  145.4 3.5 %copy-start.4 = (bf16[512,256]{1,0:T(8,128)(2,1)S(1)}, bf16[512,256]{1,0:T(8,128)(2,1)}, u32[]{:S(2)}) copy-start(bf16[512,256]{1,0:T(8,128)(2,1)} %param.14) | copy-start | bytes 786436
Sparse Core Ops, SparseCore 0:
  150.4 124.5 all-reduce.1
where the time goes:
time: 284 us
  waiting for transfers between devices  139 us (49%)
  local copies, waits for them, and re-layouts  45.8 us (16%)
  starting transfers between devices  43.4 us (15%)
  matrix products  35.9 us (13%)
  between operations  15.2 us (5%)
  other arithmetic  3.69 us (1%)
    psum x1, waiting for transfers between devices, per_device(): lax.psum(lax.dot_general(state_values, final_mixed, (((0,), (0,)), ((), (...  125 us
    ppermute x20, starting transfers between devices, passed_along(): return lax.ppermute(value, axis, pairs)  43.4 us
    unnamed x35, local copies, waits for them, and re-layouts  19.7 us
    dot_general x5, matrix products, add_tiles(): jnp.einsum('tij,tjh->tih', tiles, rows, preferred_element_type=jnp.float32)  17.2 us
    gather x20, local copies, waits for them, and re-layouts, with_boundary(): chosen = jnp.take(scaled, send_rows[direction], axis=0)  16.9 us
    dot_general x5, matrix products, add_tiles(): jnp.dot(onehot, prod.reshape(slots, size * width), precision=lax.Precisio...  15.5 us
    ppermute x20, waiting for transfers between devices, passed_along(): return lax.ppermute(value, axis, pairs)  14.8 us
    gather x5, local copies, waits for them, and re-layouts, add_tiles(): rows = jnp.take(stacked, index, axis=0)  8.06 us
  transfers between devices with their start and end apart: 21, of which 11 were waited for; matrix products, arithmetic and copies ran while one was open for 1% of the time, Pallas kernels for 0%

commit v1 on v0

--- a/solution.py
+++ b/solution.py
@@ -5,6 +5,7 @@
 
 ITERS = 4
 neighbour_steps = (1, -1, 16, -16)
+_pack_space = lambda local_values: jnp.sum(lax.all_gather(local_values, axis_name="dom"), 0)
 
 
 def passed_along(value, axis, steps):
@@ -61,12 +62,11 @@
     factor = 1.0 / jnp.sqrt(jnp.float32(node_total))
     state_values = states.astype(jnp.float32)
     final_mixed = propagate(final_scaled, tiles, tile_dst, tile_src, count, send_rows)
-    grad = lax.psum(
+    grad = _pack_space(
         lax.dot_general(
             state_values, final_mixed, (((0,), (0,)), ((), ())), precision=lax.Precision.HIGHEST
         )
-        * factor,
-        "dom",
+        * factor
     )
     return (adjoint, grad)
 

time: 284 us -> 249 us (0.88)
  waiting for transfers between devices: 139 us -> 97 us
  local copies, waits for them, and re-layouts: 45.8 us -> 51.7 us
    psum x1 -> x0, waiting for transfers between devices: 125 us -> none  [per_device(): lax.psum(lax.dot_general(state_values, final_mixed, (((0,), (0,)), ((), (...]
    all_gather x0 -> x1, waiting for transfers between devices: none -> 82.2 us  [lax.all_gather(local_values, axis_name='dom')]
    unnamed x35 -> x36, local copies, waits for them, and re-layouts: 19.7 us -> 25.6 us
where the time goes in v1:
time: 249 us
  waiting for transfers between devices  97 us (39%)
  local copies, waits for them, and re-layouts  51.7 us (21%)
  starting transfers between devices  43.4 us (17%)
  matrix products  35.9 us (14%)
  between operations  15.3 us (6%)
  other arithmetic  5.62 us (2%)
    all_gather x1, waiting for transfers between devices, lax.all_gather(local_values, axis_name='dom')  82.2 us
    ppermute x20, starting transfers between devices, passed_along(): return lax.ppermute(value, axis, pairs)  43.4 us
    unnamed x36, local copies, waits for them, and re-layouts  25.6 us
    dot_general x5, matrix products, add_tiles(): jnp.einsum('tij,tjh->tih', tiles, rows, preferred_element_type=jnp.float32)  17.2 us
    gather x20, local copies, waits for them, and re-layouts, with_boundary(): chosen = jnp.take(scaled, send_rows[direction], axis=0)  16.9 us
    dot_general x5, matrix products, add_tiles(): jnp.dot(onehot, prod.reshape(slots, size * width), precision=lax.Precisio...  15.5 us
    ppermute x20, waiting for transfers between devices, passed_along(): return lax.ppermute(value, axis, pairs)  14.8 us
    gather x5, local copies, waits for them, and re-layouts, add_tiles(): rows = jnp.take(stacked, index, axis=0)  8.06 us
  transfers between devices with their start and end apart: 21, of which 11 were waited for; matrix products, arithmetic and copies ran while one was open for 1% of the time, Pallas kernels for 0%

profile of v1, /device:TPU:0, one launch (start us, length us, event | category | flops | bytes accessed | tf_op | source)
XLA Modules:
  0.0 248.9 jit_solution(16563301579250231544)
XLA Ops:
  10.1 6.5 %collective-permute-start.1 = (bf16[128,256]{1,0:T(8,128)(2,1)S(1)}, bf16[128,256]{1,0:T(8,128)(2,1)S(1)}, u32[]{:S(2)}, u32[]{:S(2)}) collective-permute-start(bf16[128,256]{1,0:T(8,128)(2,1)S(1)} %broadcast_select_fusion.14), channel_id=1, source_target_pairs={{0,31},{1,0},{2,1},{3,2},{4,3},{5,4},{6,5},{7,6},{8,7},{9,8},{10,9... | collective-permute-start | bytes 196616 | tf_op jit(solution)/shard_map/ppermute | solution.py:14
  19.6 3.0 %collective-permute-start.3 = (bf16[128,256]{1,0:T(8,128)(2,1)S(1)}, bf16[128,256]{1,0:T(8,128)(2,1)S(1)}, u32[]{:S(2)}, u32[]{:S(2)}) collective-permute-start(bf16[128,256]{1,0:T(8,128)(2,1)S(1)} %broadcast_select_fusion.4), channel_id=1, source_target_pairs={{0,16},{1,17},{2,18},{3,19},{4,20},{5,21},{6,22},{7,23},{8,24},{9,... | collective-permute-start | bytes 196616 | tf_op jit(solution)/shard_map/ppermute | solution.py:14
  26.6 2.3 convolution_bitcast_fusion.4
  28.9 3.6 %copy.37 = f32[3,8,128,256]{3,1,2,0:T(8,128)} copy(f32[3,8,128,256]{2,3,1,0:T(8,128)} %bitcast.82) | data formatting | bytes 6291456
  32.5 3.1 %convolution_convert_fusion.3 = bf16[4,32768]{1,0:T(4,128)(2,1)S(1)} fusion(pred[4,24]{1,0:T(4,128)(4,1)S(1)} %fusion.24, f32[24,32768]{1,0:T(8,128)} %bitcast.76), kind=kOutput, calls=%fused_computation.28 | convolution fusion | flops 37879808 | bytes 3407968 | tf_op jit(solution)/shard_map/dot_general | solution.py:31
  39.9 5.4 %collective-permute-start.5 = (bf16[128,256]{1,0:T(8,128)(2,1)S(1)}, bf16[128,256]{1,0:T(8,128)(2,1)S(1)}, u32[]{:S(2)}, u32[]{:S(2)}) collective-permute-start(bf16[128,256]{1,0:T(8,128)(2,1)S(1)} %broadcast_select_fusion.13), channel_id=1, source_target_pairs={{0,31},{1,0},{2,1},{3,2},{4,3},{5,4},{6,5},{7,6},{8,7},{9,8},{10,9... | collective-permute-start | bytes 196616 | tf_op jit(solution)/shard_map/ppermute | solution.py:14
  45.4 2.9 %collective-permute-start.7 = (bf16[128,256]{1,0:T(8,128)(2,1)S(1)}, bf16[128,256]{1,0:T(8,128)(2,1)S(1)}, u32[]{:S(2)}, u32[]{:S(2)}) collective-permute-start(bf16[128,256]{1,0:T(8,128)(2,1)S(1)} %broadcast_select_fusion.3), channel_id=1, source_target_pairs={{0,16},{1,17},{2,18},{3,19},{4,20},{5,21},{6,22},{7,23},{8,24},{9,... | collective-permute-start | bytes 196616 | tf_op jit(solution)/shard_map/ppermute | solution.py:14
  48.3 2.8 %collective-permute-done.6 = bf16[128,256]{1,0:T(8,128)(2,1)S(1)} collective-permute-done((bf16[128,256]{1,0:T(8,128)(2,1)S(1)}, bf16[128,256]{1,0:T(8,128)(2,1)S(1)}, u32[]{:S(2)}, u32[]{:S(2)}) %collective-permute-start.6) | collective-permute-done | bytes 65568 | tf_op jit(solution)/shard_map/ppermute | solution.py:14
  53.6 3.7 %convolution_bitcast_fusion.3 = f32[24,128,256]{1,2,0:T(8,128)} fusion(bf16[24,128,128]{2,1,0:T(8,128)(2,1)S(1)} %copy-done, bf16[24,128,256]{2,1,0:T(8,128)(2,1)} %gather_fusion.9, pred[24]{0:T(512)(128)(4,1)S(1)} %get-tuple-element.8), kind=kOutput, calls=%fused_computation.33 | convolution fusion | flops 202113024 | bytes 5505048 | tf_op jit(solution)/shard_map/tij,tjh->tih/dot_general | solution.py:26
  57.4 3.6 %copy.38 = f32[3,8,128,256]{3,1,2,0:T(8,128)} copy(f32[3,8,128,256]{2,3,1,0:T(8,128)} %bitcast.83) | data formatting | bytes 6291456
  60.9 3.1 %convolution_convert_fusion.2 = bf16[4,32768]{1,0:T(4,128)(2,1)S(1)} fusion(pred[4,24]{1,0:T(4,128)(4,1)S(1)} %fusion.24, f32[24,32768]{1,0:T(8,128)} %bitcast.77), kind=kOutput, calls=%fused_computation.27 | convolution fusion | flops 37879808 | bytes 3407968 | tf_op jit(solution)/shard_map/dot_general | solution.py:31
  68.3 5.6 %collective-permute-start.9 = (bf16[128,256]{1,0:T(8,128)(2,1)S(1)}, bf16[128,256]{1,0:T(8,128)(2,1)S(1)}, u32[]{:S(2)}, u32[]{:S(2)}) collective-permute-start(bf16[128,256]{1,0:T(8,128)(2,1)S(1)} %broadcast_select_fusion.12), channel_id=1, source_target_pairs={{0,31},{1,0},{2,1},{3,2},{4,3},{5,4},{6,5},{7,6},{8,7},{9,8},{10,9... | collective-permute-start | bytes 196616 | tf_op jit(solution)/shard_map/ppermute | solution.py:14
  73.9 2.9 %collective-permute-start.11 = (bf16[128,256]{1,0:T(8,128)(2,1)S(1)}, bf16[128,256]{1,0:T(8,128)(2,1)S(1)}, u32[]{:S(2)}, u32[]{:S(2)}) collective-permute-start(bf16[128,256]{1,0:T(8,128)(2,1)S(1)} %broadcast_select_fusion.2), channel_id=1, source_target_pairs={{0,16},{1,17},{2,18},{3,19},{4,20},{5,21},{6,22},{7,23},{8,24},{9,... | collective-permute-start | bytes 196616 | tf_op jit(solution)/shard_map/ppermute | solution.py:14
  76.8 2.2 collective-permute-done.10
  81.6 3.7 %convolution_bitcast_fusion.2 = f32[24,128,256]{1,2,0:T(8,128)} fusion(bf16[24,128,128]{2,1,0:T(8,128)(2,1)S(1)} %copy-done, bf16[24,128,256]{2,1,0:T(8,128)(2,1)} %gather_fusion.14, pred[24]{0:T(512)(128)(4,1)S(1)} %get-tuple-element.8), kind=kOutput, calls=%fused_computation.32 | convolution fusion | flops 202113024 | bytes 5505048 | tf_op jit(solution)/shard_map/tij,tjh->tih/dot_general | solution.py:26
  85.3 3.6 %copy.39 = f32[3,8,128,256]{3,1,2,0:T(8,128)} copy(f32[3,8,128,256]{2,3,1,0:T(8,128)} %bitcast.84) | data formatting | bytes 6291456
  88.9 3.1 %convolution_convert_fusion.1 = bf16[4,32768]{1,0:T(4,128)(2,1)S(1)} fusion(pred[4,24]{1,0:T(4,128)(4,1)S(1)} %fusion.24, f32[24,32768]{1,0:T(8,128)} %bitcast.78), kind=kOutput, calls=%fused_computation.26 | convolution fusion | flops 37879808 | bytes 3407968 | tf_op jit(solution)/shard_map/dot_general | solution.py:31
  96.2 5.4 %collective-permute-start.13 = (bf16[128,256]{1,0:T(8,128)(2,1)S(1)}, bf16[128,256]{1,0:T(8,128)(2,1)S(1)}, u32[]{:S(2)}, u32[]{:S(2)}) collective-permute-start(bf16[128,256]{1,0:T(8,128)(2,1)S(1)} %broadcast_select_fusion.11), channel_id=1, source_target_pairs={{0,31},{1,0},{2,1},{3,2},{4,3},{5,4},{6,5},{7,6},{8,7},{9,8},{10,9... | collective-permute-start | bytes 196616 | tf_op jit(solution)/shard_map/ppermute | solution.py:14
  102.1 2.5 %collective-permute-start.15 = (bf16[128,256]{1,0:T(8,128)(2,1)S(1)}, bf16[128,256]{1,0:T(8,128)(2,1)S(1)}, u32[]{:S(2)}, u32[]{:S(2)}) collective-permute-start(bf16[128,256]{1,0:T(8,128)(2,1)S(1)} %broadcast_select_fusion.1), channel_id=1, source_target_pairs={{0,16},{1,17},{2,18},{3,19},{4,20},{5,21},{6,22},{7,23},{8,24},{9,... | collective-permute-start | bytes 196616 | tf_op jit(solution)/shard_map/ppermute | solution.py:14
  104.6 2.2 collective-permute-done.14
  109.4 3.7 %convolution_bitcast_fusion.1 = f32[24,128,256]{1,2,0:T(8,128)} fusion(bf16[24,128,128]{2,1,0:T(8,128)(2,1)S(1)} %copy-done, bf16[24,128,256]{2,1,0:T(8,128)(2,1)} %gather_fusion.19, pred[24]{0:T(512)(128)(4,1)S(1)} %get-tuple-element.8), kind=kOutput, calls=%fused_computation.31 | convolution fusion | flops 202113024 | bytes 5505048 | tf_op jit(solution)/shard_map/tij,tjh->tih/dot_general | solution.py:26
  113.1 3.6 %copy.40 = f32[3,8,128,256]{3,1,2,0:T(8,128)} copy(f32[3,8,128,256]{2,3,1,0:T(8,128)} %bitcast.85) | data formatting | bytes 6291456
  116.7 3.1 %convolution_convert_fusion = bf16[4,32768]{1,0:T(4,128)(2,1)S(1)} fusion(pred[4,24]{1,0:T(4,128)(4,1)S(1)} %fusion.24, f32[24,32768]{1,0:T(8,128)} %bitcast.79), kind=kOutput, calls=%fused_computation.25 | convolution fusion | flops 37879808 | bytes 3407968 | tf_op jit(solution)/shard_map/dot_general | solution.py:31
  124.8 5.6 %collective-permute-start.17 = (bf16[128,256]{1,0:T(8,128)(2,1)S(1)}, bf16[128,256]{1,0:T(8,128)(2,1)S(1)}, u32[]{:S(2)}, u32[]{:S(2)}) collective-permute-start(bf16[128,256]{1,0:T(8,128)(2,1)S(1)} %broadcast_select_fusion.10), channel_id=1, source_target_pairs={{0,31},{1,0},{2,1},{3,2},{4,3},{5,4},{6,5},{7,6},{8,7},{9,8},{10,9... | collective-permute-start | bytes 196616 | tf_op jit(solution)/shard_map/ppermute | solution.py:14
  130.8 2.5 %collective-permute-start.19 = (bf16[128,256]{1,0:T(8,128)(2,1)S(1)}, bf16[128,256]{1,0:T(8,128)(2,1)S(1)}, u32[]{:S(2)}, u32[]{:S(2)}) collective-permute-start(bf16[128,256]{1,0:T(8,128)(2,1)S(1)} %broadcast_select_fusion), channel_id=1, source_target_pairs={{0,16},{1,17},{2,18},{3,19},{4,20},{5,21},{6,22},{7,23},{8,24},{9,... | collective-permute-start | bytes 196616 | tf_op jit(solution)/shard_map/ppermute | solution.py:14
  133.4 2.2 collective-permute-done.18
  138.1 3.7 %convolution_bitcast_fusion = f32[24,128,256]{1,2,0:T(8,128)} fusion(bf16[24,128,128]{2,1,0:T(8,128)(2,1)S(1)} %copy-done, bf16[24,128,256]{2,1,0:T(8,128)(2,1)} %gather_fusion.24, pred[24]{0:T(512)(128)(4,1)S(1)} %get-tuple-element.8), kind=kOutput, calls=%fused_computation.30 | convolution fusion | flops 202113024 | bytes 5505048 | tf_op jit(solution)/shard_map/tij,tjh->tih/dot_general | solution.py:26
  141.9 3.6 %copy.41 = f32[3,8,128,256]{3,1,2,0:T(8,128)} copy(f32[3,8,128,256]{2,3,1,0:T(8,128)} %bitcast.80) | data formatting | bytes 6291456
  145.4 3.1 %fusion.32 = f32[4,32768]{1,0:T(4,128)S(1)} fusion(pred[4,24]{1,0:T(4,128)(4,1)S(1)} %fusion.24, f32[24,32768]{1,0:T(8,128)} %bitcast.81), kind=kOutput, calls=%fused_computation.134 | convolution fusion | flops 37748736 | bytes 3670112 | tf_op jit(solution)/shard_map/dot_general | solution.py:31
  150.2 82.2 %all-gather.3.cloned.1.call-done = f32[8192,256]{0,1:T(8,128)} async-done(((f32[256,256]{0,1:T(8,128)}), f32[8192,256]{0,1:T(8,128)}) %all-gather.3.cloned.1.call-update) | async-done | bytes 8388624 | tf_op jit(solution)/shard_map/all_gather | solution.py:8
  232.4 6.8 %copy.42 = f32[32,8,32,256]{3,2,1,0:T(8,128)S(1)} copy(f32[32,8,32,256]{3,1,2,0:T(8,128)} %bitcast.86) | data formatting | bytes 16777216
  239.3 1.9 bitcast_reduce_fusion
  (127 shorter events, 40.6 us)
Async XLA Ops:
  7.2 19.4 %copy-start = (bf16[24,128,128]{2,1,0:T(8,128)(2,1)S(1)}, bf16[24,128,128]{2,1,0:T(8,128)(2,1)}, u32[]{:S(2)}) copy-start(bf16[24,128,128]{2,1,0:T(8,128)(2,1)} %param.17) | copy-start | bytes 2359300
  7.2 225.2 %all-gather.3.cloned.1.call-start = ((), (), s32[]{:S(2)}) async-start(), calls=%async_computation | async-start | bytes 8650752 | tf_op jit(solution)/shard_map/all_gather | solution.py:8
  9.2 14.0 %copy-start.5 = (s32[24]{0:T(128)S(1)}, s32[24]{0:T(128)}, u32[]{:S(2)}) copy-start(s32[24]{0:T(128)} %param.19) | copy-start | bytes 292
  9.2 14.1 %copy-start.6 = (s32[24]{0:T(128)S(1)}, s32[24]{0:T(128)}, u32[]{:S(2)}) copy-start(s32[24]{0:T(128)} %param.18) | copy-start | bytes 292
  10.1 14.8 %collective-permute-start.1 = (bf16[128,256]{1,0:T(8,128)(2,1)S(1)}, bf16[128,256]{1,0:T(8,128)(2,1)S(1)}, u32[]{:S(2)}, u32[]{:S(2)}) collective-permute-start(bf16[128,256]{1,0:T(8,128)(2,1)S(1)} %broadcast_select_fusion.14), channel_id=1, source_target_pairs={{0,31},{1,0},{2,1},{3,2},{4,3},{5,4},{6,5},{7,6},{8,7},{9,8},{10,9... | collective-permute-start | bytes 196616 | tf_op jit(solution)/shard_map/ppermute | solution.py:14
  17.5 7.4 %collective-permute-start = (bf16[128,256]{1,0:T(8,128)(2,1)S(1)}, bf16[128,256]{1,0:T(8,128)(2,1)S(1)}, u32[]{:S(2)}, u32[]{:S(2)}) collective-permute-start(bf16[128,256]{1,0:T(8,128)(2,1)S(1)} %broadcast_select_fusion.19), channel_id=1, source_target_pairs={{0,1},{1,2},{2,3},{3,4},{4,5},{5,6},{6,7},{7,8},{8,9},{9,10},{10,1... | collective-permute-start | bytes 196616 | tf_op jit(solution)/shard_map/ppermute | solution.py:14
  18.6 6.4 %collective-permute-start.2 = (bf16[128,256]{1,0:T(8,128)(2,1)S(1)}, bf16[128,256]{1,0:T(8,128)(2,1)S(1)}, u32[]{:S(2)}, u32[]{:S(2)}) collective-permute-start(bf16[128,256]{1,0:T(8,128)(2,1)S(1)} %broadcast_select_fusion.9), channel_id=1, source_target_pairs={{0,16},{1,17},{2,18},{3,19},{4,20},{5,21},{6,22},{7,23},{8,24},{9,... | collective-permute-start | bytes 196616 | tf_op jit(solution)/shard_map/ppermute | solution.py:14
  19.6 6.3 %collective-permute-start.3 = (bf16[128,256]{1,0:T(8,128)(2,1)S(1)}, bf16[128,256]{1,0:T(8,128)(2,1)S(1)}, u32[]{:S(2)}, u32[]{:S(2)}) collective-permute-start(bf16[128,256]{1,0:T(8,128)(2,1)S(1)} %broadcast_select_fusion.4), channel_id=1, source_target_pairs={{0,16},{1,17},{2,18},{3,19},{4,20},{5,21},{6,22},{7,23},{8,24},{9,... | collective-permute-start | bytes 196616 | tf_op jit(solution)/shard_map/ppermute | solution.py:14
  32.5 3.3 %copy-start.1 = (bf16[512,256]{1,0:T(8,128)(2,1)S(1)}, bf16[512,256]{1,0:T(8,128)(2,1)}, u32[]{:S(2)}) copy-start(bf16[512,256]{1,0:T(8,128)(2,1)} %param.15) | copy-start | bytes 786436
  32.5 3.3 %copy-start.2 = (bf16[512,256]{1,0:T(8,128)(2,1)S(1)}, bf16[512,256]{1,0:T(8,128)(2,1)}, u32[]{:S(2)}) copy-start(bf16[512,256]{1,0:T(8,128)(2,1)} %param.13) | copy-start | bytes 786436
  32.5 3.4 %copy-start.3 = (bf16[256,256]{1,0:T(8,128)(2,1)S(1)}, bf16[256,256]{1,0:T(8,128)(2,1)}, u32[]{:S(2)}) copy-start(bf16[256,256]{1,0:T(8,128)(2,1)} %param.16) | copy-start | bytes 393220
  39.8 8.5 %collective-permute-start.4 = (bf16[128,256]{1,0:T(8,128)(2,1)S(1)}, bf16[128,256]{1,0:T(8,128)(2,1)S(1)}, u32[]{:S(2)}, u32[]{:S(2)}) collective-permute-start(bf16[128,256]{1,0:T(8,128)(2,1)S(1)} %broadcast_select_fusion.18), channel_id=1, source_target_pairs={{0,1},{1,2},{2,3},{3,4},{4,5},{5,6},{6,7},{7,8},{8,9},{9,10},{10,1... | collective-permute-start | bytes 196616 | tf_op jit(solution)/shard_map/ppermute | solution.py:14
  39.9 8.3 %collective-permute-start.5 = (bf16[128,256]{1,0:T(8,128)(2,1)S(1)}, bf16[128,256]{1,0:T(8,128)(2,1)S(1)}, u32[]{:S(2)}, u32[]{:S(2)}) collective-permute-start(bf16[128,256]{1,0:T(8,128)(2,1)S(1)} %broadcast_select_fusion.13), channel_id=1, source_target_pairs={{0,31},{1,0},{2,1},{3,2},{4,3},{5,4},{6,5},{7,6},{8,7},{9,8},{10,9... | collective-permute-start | bytes 196616 | tf_op jit(solution)/shard_map/ppermute | solution.py:14
  45.3 5.7 %collective-permute-start.6 = (bf16[128,256]{1,0:T(8,128)(2,1)S(1)}, bf16[128,256]{1,0:T(8,128)(2,1)S(1)}, u32[]{:S(2)}, u32[]{:S(2)}) collective-permute-start(bf16[128,256]{1,0:T(8,128)(2,1)S(1)} %broadcast_select_fusion.8), channel_id=1, source_target_pairs={{0,16},{1,17},{2,18},{3,19},{4,20},{5,21},{6,22},{7,23},{8,24},{9,... | collective-permute-start | bytes 196616 | tf_op jit(solution)/shard_map/ppermute | solution.py:14
  45.4 6.4 %collective-permute-start.7 = (bf16[128,256]{1,0:T(8,128)(2,1)S(1)}, bf16[128,256]{1,0:T(8,128)(2,1)S(1)}, u32[]{:S(2)}, u32[]{:S(2)}) collective-permute-start(bf16[128,256]{1,0:T(8,128)(2,1)S(1)} %broadcast_select_fusion.3), channel_id=1, source_target_pairs={{0,16},{1,17},{2,18},{3,19},{4,20},{5,21},{6,22},{7,23},{8,24},{9,... | collective-permute-start | bytes 196616 | tf_op jit(solution)/shard_map/ppermute | solution.py:14
  68.1 8.6 %collective-permute-start.8 = (bf16[128,256]{1,0:T(8,128)(2,1)S(1)}, bf16[128,256]{1,0:T(8,128)(2,1)S(1)}, u32[]{:S(2)}, u32[]{:S(2)}) collective-permute-start(bf16[128,256]{1,0:T(8,128)(2,1)S(1)} %broadcast_select_fusion.17), channel_id=1, source_target_pairs={{0,1},{1,2},{2,3},{3,4},{4,5},{5,6},{6,7},{7,8},{8,9},{9,10},{10,1... | collective-permute-start | bytes 196616 | tf_op jit(solution)/shard_map/ppermute | solution.py:14
  68.3 8.5 %collective-permute-start.9 = (bf16[128,256]{1,0:T(8,128)(2,1)S(1)}, bf16[128,256]{1,0:T(8,128)(2,1)S(1)}, u32[]{:S(2)}, u32[]{:S(2)}) collective-permute-start(bf16[128,256]{1,0:T(8,128)(2,1)S(1)} %broadcast_select_fusion.12), channel_id=1, source_target_pairs={{0,31},{1,0},{2,1},{3,2},{4,3},{5,4},{6,5},{7,6},{8,7},{9,8},{10,9... | collective-permute-start | bytes 196616 | tf_op jit(solution)/shard_map/ppermute | solution.py:14
  73.9 5.2 %collective-permute-start.10 = (bf16[128,256]{1,0:T(8,128)(2,1)S(1)}, bf16[128,256]{1,0:T(8,128)(2,1)S(1)}, u32[]{:S(2)}, u32[]{:S(2)}) collective-permute-start(bf16[128,256]{1,0:T(8,128)(2,1)S(1)} %broadcast_select_fusion.7), channel_id=1, source_target_pairs={{0,16},{1,17},{2,18},{3,19},{4,20},{5,21},{6,22},{7,23},{8,24},{9,... | collective-permute-start | bytes 196616 | tf_op jit(solution)/shard_map/ppermute | solution.py:14
  73.9 5.9 %collective-permute-start.11 = (bf16[128,256]{1,0:T(8,128)(2,1)S(1)}, bf16[128,256]{1,0:T(8,128)(2,1)S(1)}, u32[]{:S(2)}, u32[]{:S(2)}) collective-permute-start(bf16[128,256]{1,0:T(8,128)(2,1)S(1)} %broadcast_select_fusion.2), channel_id=1, source_target_pairs={{0,16},{1,17},{2,18},{3,19},{4,20},{5,21},{6,22},{7,23},{8,24},{9,... | collective-permute-start | bytes 196616 | tf_op jit(solution)/shard_map/ppermute | solution.py:14
  96.1 8.5 %collective-permute-start.12 = (bf16[128,256]{1,0:T(8,128)(2,1)S(1)}, bf16[128,256]{1,0:T(8,128)(2,1)S(1)}, u32[]{:S(2)}, u32[]{:S(2)}) collective-permute-start(bf16[128,256]{1,0:T(8,128)(2,1)S(1)} %broadcast_select_fusion.16), channel_id=1, source_target_pairs={{0,1},{1,2},{2,3},{3,4},{4,5},{5,6},{6,7},{7,8},{8,9},{9,10},{10,1... | collective-permute-start | bytes 196616 | tf_op jit(solution)/shard_map/ppermute | solution.py:14
  96.2 8.3 %collective-permute-start.13 = (bf16[128,256]{1,0:T(8,128)(2,1)S(1)}, bf16[128,256]{1,0:T(8,128)(2,1)S(1)}, u32[]{:S(2)}, u32[]{:S(2)}) collective-permute-start(bf16[128,256]{1,0:T(8,128)(2,1)S(1)} %broadcast_select_fusion.11), channel_id=1, source_target_pairs={{0,31},{1,0},{2,1},{3,2},{4,3},{5,4},{6,5},{7,6},{8,7},{9,8},{10,9... | collective-permute-start | bytes 196616 | tf_op jit(solution)/shard_map/ppermute | solution.py:14
  101.6 5.2 %collective-permute-start.14 = (bf16[128,256]{1,0:T(8,128)(2,1)S(1)}, bf16[128,256]{1,0:T(8,128)(2,1)S(1)}, u32[]{:S(2)}, u32[]{:S(2)}) collective-permute-start(bf16[128,256]{1,0:T(8,128)(2,1)S(1)} %broadcast_select_fusion.6), channel_id=1, source_target_pairs={{0,16},{1,17},{2,18},{3,19},{4,20},{5,21},{6,22},{7,23},{8,24},{9,... | collective-permute-start | bytes 196616 | tf_op jit(solution)/shard_map/ppermute | solution.py:14
  102.1 5.4 %collective-permute-start.15 = (bf16[128,256]{1,0:T(8,128)(2,1)S(1)}, bf16[128,256]{1,0:T(8,128)(2,1)S(1)}, u32[]{:S(2)}, u32[]{:S(2)}) collective-permute-start(bf16[128,256]{1,0:T(8,128)(2,1)S(1)} %broadcast_select_fusion.1), channel_id=1, source_target_pairs={{0,16},{1,17},{2,18},{3,19},{4,20},{5,21},{6,22},{7,23},{8,24},{9,... | collective-permute-start | bytes 196616 | tf_op jit(solution)/shard_map/ppermute | solution.py:14
  124.6 8.7 %collective-permute-start.16 = (bf16[128,256]{1,0:T(8,128)(2,1)S(1)}, bf16[128,256]{1,0:T(8,128)(2,1)S(1)}, u32[]{:S(2)}, u32[]{:S(2)}) collective-permute-start(bf16[128,256]{1,0:T(8,128)(2,1)S(1)} %broadcast_select_fusion.15), channel_id=1, source_target_pairs={{0,1},{1,2},{2,3},{3,4},{4,5},{5,6},{6,7},{7,8},{8,9},{9,10},{10,1... | collective-permute-start | bytes 196616 | tf_op jit(solution)/shard_map/ppermute | solution.py:14
  124.8 8.5 %collective-permute-start.17 = (bf16[128,256]{1,0:T(8,128)(2,1)S(1)}, bf16[128,256]{1,0:T(8,128)(2,1)S(1)}, u32[]{:S(2)}, u32[]{:S(2)}) collective-permute-start(bf16[128,256]{1,0:T(8,128)(2,1)S(1)} %broadcast_select_fusion.10), channel_id=1, source_target_pairs={{0,31},{1,0},{2,1},{3,2},{4,3},{5,4},{6,5},{7,6},{8,7},{9,8},{10,9... | collective-permute-start | bytes 196616 | tf_op jit(solution)/shard_map/ppermute | solution.py:14
  130.4 5.2 %collective-permute-start.18 = (bf16[128,256]{1,0:T(8,128)(2,1)S(1)}, bf16[128,256]{1,0:T(8,128)(2,1)S(1)}, u32[]{:S(2)}, u32[]{:S(2)}) collective-permute-start(bf16[128,256]{1,0:T(8,128)(2,1)S(1)} %broadcast_select_fusion.5), channel_id=1, source_target_pairs={{0,16},{1,17},{2,18},{3,19},{4,20},{5,21},{6,22},{7,23},{8,24},{9,... | collective-permute-start | bytes 196616 | tf_op jit(solution)/shard_map/ppermute | solution.py:14
  130.8 5.4 %collective-permute-start.19 = (bf16[128,256]{1,0:T(8,128)(2,1)S(1)}, bf16[128,256]{1,0:T(8,128)(2,1)S(1)}, u32[]{:S(2)}, u32[]{:S(2)}) collective-permute-start(bf16[128,256]{1,0:T(8,128)(2,1)S(1)} %broadcast_select_fusion), channel_id=1, source_target_pairs={{0,16},{1,17},{2,18},{3,19},{4,20},{5,21},{6,22},{7,23},{8,24},{9,... | collective-permute-start | bytes 196616 | tf_op jit(solution)/shard_map/ppermute | solution.py:14
  145.4 3.5 %copy-start.4 = (bf16[512,256]{1,0:T(8,128)(2,1)S(1)}, bf16[512,256]{1,0:T(8,128)(2,1)}, u32[]{:S(2)}) copy-start(bf16[512,256]{1,0:T(8,128)(2,1)} %param.14) | copy-start | bytes 786436
Sparse Core Ops, SparseCore 0:
  150.4 82.0 all-gather.2
